TPU v7x, 32 devices: a whole 2x2x4 slice. The times are simulated.
32 devices in a mesh: groups: 2 (over y), seq: 4 (over x, core), tensor: 4 (over z).
Axes of the slice: x: 2, y: 2, z: 4, core: 2. Of those that a mesh axis runs over, the one named last changes fastest.
Arguments:
- patches: bfloat16 [2056, 1280], P(('groups', 'seq')), parts along dimension 0, may hold values from -6 to 6
- latents: bfloat16 [64, 1280], replicated, may hold values from -160 to 160
- wq_res: bfloat16 [1280, 1536], P(None, 'tensor'), may hold values from -0.15625 to 0.15625
- wk_res: bfloat16 [1280, 1536], P(None, 'tensor'), may hold values from -0.3125 to 0.3125
- wv_res: bfloat16 [1280, 1536], P(None, 'tensor'), may hold values from -0.15625 to 0.15625
- wo_res: bfloat16 [1536, 1280], P('tensor'), may hold values from -0.625 to 0.625
- text: bfloat16 [3072, 8192], P('groups', 'seq'), parts along dimension 0, may hold values from -240 to 240
- norm_gain: bfloat16 [8192], P('seq'), may hold values from 0.25 to 1.75
- wq_x: bfloat16 [8192, 8192], P('seq', 'tensor'), may hold values from -0.0625 to 0.0625
- wk_x: bfloat16 [1280, 8192], P(None, 'tensor'), may hold values from -0.15625 to 0.15625
- wv_x: bfloat16 [1280, 8192], P(None, 'tensor'), may hold values from -0.15625 to 0.15625
- wo_x: bfloat16 [8192, 8192], P('tensor', 'seq'), may hold values from -0.25 to 0.25
- gate_x: float32 [8192], P('seq'), may hold values from -1.5 to 1.5
- text_image: int32 [3072], P('groups'), parts along dimension 0, may hold values from -1 to 3, as said below
Outputs:
- text_out: float32 [3072, 8192], P('groups', 'seq'), parts along dimension 0
- page_latents: bfloat16 [512, 1280], P(('groups', 'seq')), parts along dimension 0
There are 2 independent parts, one for each index of `groups`. A program takes and returns all parts, laid end to end along the dimension named above; an argument that names none is the same for every part. Nothing has to cross between parts.
Inputs may be any that keep to these rules, and one draw needn't show every extreme that they name: text_image[t] is the index of the last image placed at or before token t, -1 before the first image; it never falls along the tokens, and every one of the 4 images is the value of some tokens.
All inputs are finite; a program needn't handle non-finite values.
Results may differ from a plain program's by a relative error of at most 0.015.
The roundings to bfloat16 on the way count: a program that leaves them out, or rounds other values in their place, can miss the bound.
Values may be sent and summed in bfloat16 or wider, within the bound.
A program may use at most 192 MiB of HBM per device.

v0:
```python
import math
import jax
import jax.numpy as jnp
from jax import lax
from jax.sharding import PartitionSpec as P

WIDTH = 8192
HEAD = 128
RES_HEAD = 96
PATCH_IMG = 257


def shards(
    patches,
    latents,
    wq_res,
    wk_res,
    wv_res,
    wo_res,
    text,
    norm_gain,
    wq_x,
    wk_x,
    wv_x,
    wo_x,
    gate_x,
    text_image,
):
    inv_res = 1.0 / math.sqrt(RES_HEAD)
    inv_root = 1.0 / math.sqrt(HEAD)
    lat_count = latents.shape[0]
    img_count = patches.shape[0] // PATCH_IMG
    heads_res = wq_res.shape[1] // RES_HEAD
    queries = (
        jnp.dot(latents, wq_res, preferred_element_type=jnp.float32)
        .astype(jnp.bfloat16)
        .reshape(lat_count, heads_res, RES_HEAD)
    )
    page_keys = (
        jnp.dot(patches, wk_res, preferred_element_type=jnp.float32)
        .astype(jnp.bfloat16)
        .reshape(img_count, PATCH_IMG, heads_res, RES_HEAD)
    )
    page_values = (
        jnp.dot(patches, wv_res, preferred_element_type=jnp.float32)
        .astype(jnp.bfloat16)
        .reshape(img_count, PATCH_IMG, heads_res, RES_HEAD)
    )
    scores = (
        jnp.einsum("lhd,iphd->ihlp", queries, page_keys, preferred_element_type=jnp.float32)
        * inv_res
    )
    summit = jnp.max(scores, axis=3, keepdims=True)
    weights = jnp.exp(scores - summit).astype(jnp.bfloat16)
    totals = jnp.sum(weights, axis=3, dtype=jnp.float32)
    blended = jnp.einsum(
        "ihlp,iphd->ihld", weights, page_values, preferred_element_type=jnp.float32
    )
    pooled = (
        (blended / totals[:, :, :, None])
        .transpose(0, 2, 1, 3)
        .reshape(img_count * lat_count, heads_res * RES_HEAD)
        .astype(jnp.bfloat16)
    )
    partial_value = jnp.dot(pooled, wo_res, preferred_element_type=jnp.float32)
    latent_sum = lax.psum(partial_value, "tensor")
    repeated = jnp.tile(latents, (img_count, 1)).astype(jnp.float32)
    page_latents = (repeated + latent_sum).astype(jnp.bfloat16)
    tok_count = text.shape[0]
    hidden = text.astype(jnp.float32)
    squares = jnp.sum(hidden * hidden, axis=1)
    scaled = (hidden * norm_gain.astype(jnp.float32)).astype(jnp.bfloat16)
    query_part = jnp.dot(scaled, wq_x, preferred_element_type=jnp.float32)
    squares, query_sum = lax.psum((squares, query_part), "seq")
    inverse = lax.rsqrt(squares / WIDTH + 1e-05)
    heads_x = wq_x.shape[1] // HEAD
    text_queries = (query_sum * inverse[:, None]).astype(jnp.bfloat16)
    own_keys = jnp.dot(page_latents, wk_x, preferred_element_type=jnp.float32).astype(jnp.bfloat16)
    own_values = jnp.dot(page_latents, wv_x, preferred_element_type=jnp.float32).astype(
        jnp.bfloat16
    )
    cross_keys, cross_values = (
        lax.all_gather(own_keys, "seq", axis=0, tiled=True),
        lax.all_gather(own_values, "seq", axis=0, tiled=True),
    )
    lat_all = cross_keys.shape[0]
    cross_keys = cross_keys.reshape(lat_all, heads_x, HEAD)
    cross_values = cross_values.reshape(lat_all, heads_x, HEAD)
    latent_owner = jnp.arange(lat_all, dtype=jnp.int32) // lat_count
    row_block = math.gcd(tok_count, 512)
    n_blocks = tok_count // row_block
    q_blocks = text_queries.reshape(n_blocks, row_block, heads_x, HEAD)
    img_blocks = text_image.reshape(n_blocks, row_block)

    def attend(inputs):
        q_rows, img_rows = inputs
        logits = (
            jnp.einsum("thd,lhd->htl", q_rows, cross_keys, preferred_element_type=jnp.float32)
            * inv_root
        )
        allowed = img_rows[:, None] == latent_owner[None, :]
        logits = jnp.where(allowed[None, :, :], logits, -1e30)
        row_peak = jnp.max(logits, axis=2, keepdims=True)
        probs_bf = jnp.exp(logits - row_peak).astype(jnp.bfloat16)
        row_total = jnp.sum(probs_bf, axis=2, dtype=jnp.float32)
        mixture = jnp.einsum(
            "htl,lhd->thd", probs_bf, cross_values, preferred_element_type=jnp.float32
        )
        visible = (img_rows >= 0).astype(jnp.float32)
        return (mixture / row_total.T[:, :, None] * visible[:, None, None]).astype(jnp.bfloat16)

    attended = lax.map(attend, (q_blocks, img_blocks)).reshape(tok_count, heads_x * HEAD)
    block_part = jnp.dot(attended, wo_x, preferred_element_type=jnp.float32)
    gate_open = jnp.tanh(gate_x)
    block_whole = lax.psum(block_part.astype(jnp.bfloat16), "tensor").astype(jnp.float32)
    text_out = hidden + gate_open * block_whole
    return (text_out, page_latents)


def solution(mesh):
    in_specs = (
        P(("groups", "seq"), None),
        P(),
        P(None, "tensor"),
        P(None, "tensor"),
        P(None, "tensor"),
        P("tensor", None),
        P("groups", "seq"),
        P("seq"),
        P("seq", "tensor"),
        P(None, "tensor"),
        P(None, "tensor"),
        P("tensor", "seq"),
        P("seq"),
        P("groups"),
    )
    out_specs = (P("groups", "seq"), P(("groups", "seq"), None))
    return jax.shard_map(shards, mesh=mesh, in_specs=in_specs, out_specs=out_specs, check_vma=False)
```

profile of v0, /device:TPU:0, one launch (start us, length us, event | category | flops | bytes accessed | tf_op | source)
XLA Modules:
  0.0 635.0 jit_solution(5875707518718355605)
XLA Ops:
  7.2 0.0 copy-start
  7.2 0.0 copy-start.4
  7.2 0.0 all-reduce.6.cloned.1.call-start
  7.2 1.4 copy-done
  8.7 1.6 convolution_convert_fusion.4
  10.3 0.3 reshape.96
  10.6 1.6 convolution_convert_fusion.5
  12.2 0.1 reshape.97
  12.3 1.9 convolution_convert_fusion.3
  14.2 0.3 reshape.99
  14.6 0.3 fusion.24
  14.9 0.2 convert_reduce_fusion.1
  15.1 0.3 fusion.19
  15.4 0.1 copy.27
  15.5 0.1 convert_element_type.86
  15.6 1.0 fusion.25
  16.6 0.0 all-reduce.6.cloned.1.call-update
  16.6 0.0 all-gather.5.cloned.1.call-start
  16.7 39.3 %all-reduce.6.cloned.1.call-done = f32[64,1280]{1,0:T(8,128)} async-done(((f32[64,1280]{1,0:T(8,128)}), f32[64,1280]{1,0:T(8,128)}) %all-reduce.6.cloned.1.call-update) | async-done | bytes 327696 | tf_op jit(solution)/shard_map/psum | solution.py:66
  55.9 1.0 add_convert_fusion
  56.9 0.0 copy-start.2
  56.9 4.3 convolution_convert_fusion.1
  61.2 0.0 all-gather.5.cloned.1.call-update
  61.2 0.0 all-gather.3.cloned.1.call-start
  61.3 4.2 convolution_convert_fusion.2
  65.5 0.0 all-gather.3.cloned.1.call-update
  65.5 0.0 all-reduce.4.cloned.1.call-start
  65.6 19.3 %fusion.12 = f32[1536,2048]{1,0:T(8,128)} fusion(bf16[2048,2048]{1,0:T(8,128)(2,1)} %param.24, bf16[1536,2048]{1,0:T(8,128)(2,1)} %param.22, f32[2048]{0:T(1024)S(1)} %convert_element_type.74), kind=kOutput, calls=%fused_computation.30 | convolution fusion | flops 12894339072 | bytes 27271168 | tf_op jit(solution)/shard_map/dot_general | solution.py:73
  84.9 0.0 all-reduce.4.cloned.1.call-update
  84.9 0.0 all-reduce.8.cloned.1.call-start
  84.9 0.6 copy-done.5
  85.6 4.3 fusion.10
  89.9 6.4 %psum.29 = f32[1536]{0:T(1024)S(1)} all-reduce(f32[1536]{0:T(1024)S(1)} %fusion.10), channel_id=1, replica_groups=mesh['groups'=2,'seq'=4,'tensor'=4] {'seq'}, use_global_device_ids=true, to_apply=%region_2.0 | all-reduce | flops 1536 | bytes 12288 | tf_op jit(solution)/shard_map/psum | solution.py:74
  96.3 0.0 all-gather.5.cloned.1.call-done
  96.3 1.5 copy_bitcast_fusion.2
  97.8 0.0 all-gather.3.cloned.1.call-done
  97.8 1.5 copy_bitcast_fusion.3
  99.3 220.7 %all-reduce.4.cloned.1.call-done = f32[1536,2048]{1,0:T(8,128)} async-done(((f32[1536,2048]{1,0:T(8,128)}), f32[1536,2048]{1,0:T(8,128)}) %all-reduce.4.cloned.1.call-update) | async-done | bytes 12582928 | tf_op jit(solution)/shard_map/psum | solution.py:74
  320.0 8.4 %fusion.11 = bf16[192,8,16,128]{3,1,2,0:T(8,128)(2,1)} fusion(f32[1536,2048]{1,0:T(8,128)} %all-reduce.4.cloned.1.call-done, f32[1536]{0:T(1024)S(1)} %add_rsqrt_fusion), kind=kLoop, calls=%fused_computation.29 | loop fusion | flops 6291456 | bytes 18880512
  328.4 7.8 %copy.38 = bf16[192,8,16,128]{3,2,1,0:T(8,128)(2,1)} copy(bf16[192,8,16,128]{3,1,2,0:T(8,128)(2,1)} %fusion.11) | data formatting | bytes 12582912
  336.1 37.6 %while.11 = (s32[]{:T(128)}, bf16[3,512,16,128]{3,2,1,0:T(8,128)(2,1)}, s32[3,512]{1,0:T(4,128)S(1)}, bf16[3,512,16,128]{3,2,1,0:T(8,128)(2,1)}, bf16[256,16,128...) while((s32[]{:T(128)}, bf16[3,512,16,128]{3,2,1,0:T(8,128)(2,1)}, ...), condition=%wide.region_9.10_spmd.clone, body=%wide.region_6.9_spmd.clone.sunk | while | flops 1104268288 | bytes 40548948 | solution.py:112
  336.2 0.1 broadcast_compare_fusion.2
  336.3 2.0 constant_dynamic-slice_fusion.5
  338.3 2.4 fusion.50
  340.7 1.8 convert_reduce_fusion.3
  342.5 3.5 fusion.51
  346.0 2.7 copy_dynamic-update-slice_fusion.2
  348.7 0.1 broadcast_compare_fusion.2
  348.9 2.0 constant_dynamic-slice_fusion.5
  350.8 2.4 fusion.50
  353.2 1.8 convert_reduce_fusion.3
  355.1 3.5 fusion.51
  358.5 2.7 copy_dynamic-update-slice_fusion.2
  361.2 0.1 broadcast_compare_fusion.2
  361.4 2.0 constant_dynamic-slice_fusion.5
  363.3 2.4 fusion.50
  365.7 1.8 convert_reduce_fusion.3
  367.6 3.5 fusion.51
  371.0 2.7 copy_dynamic-update-slice_fusion.2
  373.8 18.9 %convolution_convert_fusion = bf16[1536,2048]{1,0:T(8,128)(2,1)} fusion(bf16[2048,2048]{1,0:T(8,128)(2,1)} %param.27, bf16[192,8,16,128]{3,2,1,0:T(8,128)(2,1)} %bitcast.20), kind=kOutput, calls=%fused_computation.28 | convolution fusion | flops 12888047616 | bytes 20971520 | tf_op jit(solution)/shard_map/dot_general | solution.py:113
  392.6 0.0 all-reduce.8.cloned.1.call-update
  392.7 0.7 copy-done.6
  393.3 222.5 %all-reduce.8.cloned.1.call-done = bf16[1536,2048]{1,0:T(8,128)(2,1)} async-done(((bf16[1536,2048]{1,0:T(8,128)(2,1)}), bf16[1536,2048]{1,0:T(8,128)(2,1)}) %all-reduce.8.cloned.1.call-update) | async-done | bytes 6291472 | tf_op jit(solution)/shard_map/psum | solution.py:115
  615.9 12.6 %convert_add_fusion = f32[1536,2048]{1,0:T(8,128)} fusion(bf16[1536,2048]{1,0:T(8,128)(2,1)} %param.22, bf16[1536,2048]{1,0:T(8,128)(2,1)} %all-reduce.8.cloned.1.call-done, f32[2048]{0:T(1024)S(1)} %tanh.3), kind=kLoop, calls=%fused_computation.22 | loop fusion | flops 12582912 | bytes 25174016 | tf_op jit(solution)/shard_map/add | solution.py:116
  (24 shorter events, 0.1 us)
Async XLA Ops:
  7.2 1.5 copy-start
  7.2 48.7 %copy-start.4 = (bf16[64,1280]{1,0:T(8,128)(2,1)S(1)}, bf16[64,1280]{1,0:T(8,128)(2,1)}, u32[]{:S(2)}) copy-start(bf16[64,1280]{1,0:T(8,128)(2,1)} %param.17) | copy-start | bytes 491524
  7.2 8.4 %copy-start.3 = (bf16[384,1280]{1,0:T(8,128)(2,1)S(1)}, bf16[384,1280]{1,0:T(8,128)(2,1)}, u32[]{:S(2)}) copy-start(bf16[384,1280]{1,0:T(8,128)(2,1)} %param.21) | copy-start | bytes 2949124
  7.2 48.7 %all-reduce.6.cloned.1.call-start = ((), (), s32[]{:S(2)}) async-start(), calls=%async_computation.1 | async-start | bytes 655360 | tf_op jit(solution)/shard_map/psum | solution.py:66
  12.3 49.0 %copy-start.7 = (bf16[2048]{0:T(1024)(128)(2,1)S(1)}, bf16[2048]{0:T(1024)(128)(2,1)}, u32[]{:S(2)}) copy-start(bf16[2048]{0:T(1024)(128)(2,1)} %param.23) | copy-start | bytes 12292
  16.6 79.7 %all-gather.5.cloned.1.call-start = ((), (), s32[]{:S(2)}) async-start(), calls=%async_computation.3 | async-start | bytes 1310720 | tf_op jit(solution)/shard_map/all_gather | solution.py:84
  56.9 27.9 %copy-start.2 = (bf16[64,1280]{1,0:T(8,128)(2,1)}, bf16[64,1280]{1,0:T(8,128)(2,1)S(1)}, u32[]{:S(2)}) copy-start(bf16[64,1280]{1,0:T(8,128)(2,1)S(1)} %add_convert_fusion) | copy-start | bytes 491524
  61.2 36.6 %all-gather.3.cloned.1.call-start = ((), (), s32[]{:S(2)}) async-start(), calls=%async_computation.2 | async-start | bytes 1310720 | tf_op jit(solution)/shard_map/all_gather | solution.py:83
  65.5 254.5 %all-reduce.4.cloned.1.call-start = ((), (), s32[]{:S(2)}) async-start(), calls=%async_computation | async-start | bytes 25165824 | tf_op jit(solution)/shard_map/psum | solution.py:74
  84.9 0.7 copy-start.5
  84.9 531.0 %all-reduce.8.cloned.1.call-start = ((), (), s32[]{:S(2)}) async-start(), calls=%async_computation.4 | async-start | bytes 12582912 | tf_op jit(solution)/shard_map/psum | solution.py:115
  392.6 0.7 copy-start.6
  615.9 12.6 %copy-start.1 = (bf16[1280,384]{1,0:T(8,128)(2,1)S(1)}, bf16[1280,384]{1,0:T(8,128)(2,1)}, u32[]{:S(2)}) copy-start(bf16[1280,384]{1,0:T(8,128)(2,1)} %param.19) | copy-start | bytes 2949124
Sparse Core Ops, SparseCore 0:
  16.7 39.1 all-reduce.5
  61.4 16.4 all-gather.4
  79.4 16.8 all-gather.2
  99.2 220.7 all-reduce.3
  392.8 223.0 all-reduce.7
where the time goes:
time: 636 us; the launch traced here: 635 us
  waiting for transfers between devices  483 us (76%)
  matrix products  70.9 us (11%)
  other arithmetic  32.4 us (5%)
  local copies, waits for them, and re-layouts  28.4 us (4%)
  between operations  14 us (2%)
  blocking collectives  6.37 us (1%)
    psum x1, waiting for transfers between devices, shards(): lax.psum(block_part.astype(jnp.bfloat16), 'tensor').astype(jnp.float32)  223 us
    psum x1, waiting for transfers between devices, shards(): squares, query_sum = lax.psum((squares, query_part), 'seq')  221 us
    psum x1, waiting for transfers between devices, shards(): latent_sum = lax.psum(partial_value, 'tensor')  39.3 us
    dot_general x1, matrix products, shards(): query_part = jnp.dot(scaled, wq_x, preferred_element_type=jnp.float32)  19.3 us
    dot_general x1, matrix products, shards(): block_part = jnp.dot(attended, wo_x, preferred_element_type=jnp.float32)  18.9 us
    unnamed x19, local copies, waits for them, and re-layouts  13.5 us
  transfers between devices with their start and end apart: 5, of which 3 were waited for; matrix products, arithmetic and copies ran while one was open for 5% of the time, Pallas kernels for 0%

commit v1 on v0

--- a/solution.py
+++ b/solution.py
@@ -63,7 +63,11 @@
         .astype(jnp.bfloat16)
     )
     partial_value = jnp.dot(pooled, wo_res, preferred_element_type=jnp.float32)
-    latent_sum = lax.psum(partial_value, "tensor")
+    latent_sum = partial_value
+    for hop in (1, 2):
+        latent_sum = latent_sum + lax.ppermute(
+            latent_sum, "tensor", [(dev, dev ^ hop) for dev in range(4)]
+        )
     repeated = jnp.tile(latents, (img_count, 1)).astype(jnp.float32)
     page_latents = (repeated + latent_sum).astype(jnp.bfloat16)
     tok_count = text.shape[0]

time: 636 us -> 624 us (0.981)
  waiting for transfers between devices: 483 us -> 466 us
    psum x1 -> x0, waiting for transfers between devices: 39.3 us -> none  [shards(): latent_sum = lax.psum(partial_value, 'tensor')]
    ppermute x0 -> x2, waiting for transfers between devices: none -> 21.8 us  [shards(): lax.ppermute(latent_sum, 'tensor', [(dev, dev ^ hop) for dev in range(4)])]
  transfers between devices with their start and end apart: 5 -> 6, of which waited for: 3 -> 4; matrix products, arithmetic and copies ran while one was open for 5% -> 5% of each run, Pallas kernels for 0% -> 0%
where the time goes in v1:
time: 624 us; the launch traced here: 623 us
  waiting for transfers between devices  466 us (75%)
  matrix products  69.9 us (11%)
  other arithmetic  31.4 us (5%)
  local copies, waits for them, and re-layouts  28.4 us (5%)
  between operations  14 us (2%)
  blocking collectives  6.62 us (1%)
    psum x1, waiting for transfers between devices, shards(): lax.psum(block_part.astype(jnp.bfloat16), 'tensor').astype(jnp.float32)  223 us
    psum x1, waiting for transfers between devices, shards(): squares, query_sum = lax.psum((squares, query_part), 'seq')  222 us
    ppermute x2, waiting for transfers between devices, shards(): lax.ppermute(latent_sum, 'tensor', [(dev, dev ^ hop) for dev in range(4)])  21.8 us
    dot_general x1, matrix products, shards(): query_part = jnp.dot(scaled, wq_x, preferred_element_type=jnp.float32)  19 us
    dot_general x1, matrix products, shards(): block_part = jnp.dot(attended, wo_x, preferred_element_type=jnp.float32)  18.9 us
    unnamed x19, local copies, waits for them, and re-layouts  13.5 us
    add x1, other arithmetic, shards(): text_out = hidden + gate_open * block_whole  12.6 us
  transfers between devices with their start and end apart: 6, of which 4 were waited for; matrix products, arithmetic and copies ran while one was open for 5% of the time, Pallas kernels for 0%

profile of v1, /device:TPU:0, one launch (start us, length us, event | category | flops | bytes accessed | tf_op | source)
XLA Modules:
  0.0 623.0 jit_solution(2080105175972817407)
XLA Ops:
  7.2 0.0 copy-start
  7.2 0.0 all-gather.5.cloned.1.call-start
  7.2 1.4 copy-done
  8.7 1.6 convolution_convert_fusion.4
  10.3 0.3 reshape.96
  10.6 1.6 convolution_convert_fusion.5
  12.2 0.1 reshape.97
  12.3 1.9 convolution_convert_fusion.3
  14.2 0.3 reshape.99
  14.6 0.3 fusion.24
  14.9 0.2 convert_reduce_fusion.1
  15.1 0.3 fusion.19
  15.4 0.1 copy.27
  15.5 0.1 convert_element_type.86
  15.6 0.3 fusion.25
  15.8 3.1 collective-permute-start
  19.0 7.7 %collective-permute-done = f32[64,1280]{1,0:T(8,128)S(1)} collective-permute-done((f32[64,1280]{1,0:T(8,128)S(1)}, f32[64,1280]{1,0:T(8,128)S(1)}, u32[]{:S(2)}, u32[]{:S(2)}) %collective-permute-start) | collective-permute-done | bytes 327712 | tf_op jit(solution)/shard_map/ppermute | solution.py:68
  26.7 2.8 collective-permute-start.1
  29.5 14.0 %collective-permute-done.1 = f32[64,1280]{1,0:T(8,128)S(1)} collective-permute-done((f32[64,1280]{1,0:T(8,128)S(1)}, f32[64,1280]{1,0:T(8,128)S(1)}, u32[]{:S(2)}, u32[]{:S(2)}) %collective-permute-start.1) | collective-permute-done | bytes 327712 | tf_op jit(solution)/shard_map/ppermute | solution.py:68
  43.6 0.1 add_convert_fusion
  43.6 0.0 copy-start.2
  43.6 4.3 convolution_convert_fusion.1
  47.9 0.0 all-gather.5.cloned.1.call-update
  47.9 0.0 all-gather.3.cloned.1.call-start
  48.0 4.2 convolution_convert_fusion.2
  52.2 0.0 all-gather.3.cloned.1.call-update
  52.2 0.0 all-reduce.3.cloned.1.call-start
  52.3 19.0 %fusion.12 = f32[1536,2048]{1,0:T(8,128)} fusion(bf16[2048,2048]{1,0:T(8,128)(2,1)} %param.24, bf16[1536,2048]{1,0:T(8,128)(2,1)} %param.22, f32[2048]{0:T(1024)S(1)} %convert_element_type.74), kind=kOutput, calls=%fused_computation.30 | convolution fusion | flops 12894339072 | bytes 27271168 | tf_op jit(solution)/shard_map/dot_general | solution.py:77
  71.3 0.0 all-reduce.3.cloned.1.call-update
  71.3 0.0 all-reduce.5.cloned.1.call-start
  71.4 0.6 copy-done.5
  72.0 4.3 fusion.10
  76.3 6.6 %psum.22 = f32[1536]{0:T(1024)S(1)} all-reduce(f32[1536]{0:T(1024)S(1)} %fusion.10), channel_id=1, replica_groups=mesh['groups'=2,'seq'=4,'tensor'=4] {'seq'}, use_global_device_ids=true, to_apply=%region_2.0 | all-reduce | flops 1536 | bytes 12288 | tf_op jit(solution)/shard_map/psum | solution.py:78
  82.9 0.0 all-gather.5.cloned.1.call-done
  83.0 1.5 copy_bitcast_fusion.2
  84.5 0.0 all-gather.3.cloned.1.call-done
  84.5 1.5 copy_bitcast_fusion.3
  86.0 222.0 %all-reduce.3.cloned.1.call-done = f32[1536,2048]{1,0:T(8,128)} async-done(((f32[1536,2048]{1,0:T(8,128)}), f32[1536,2048]{1,0:T(8,128)}) %all-reduce.3.cloned.1.call-update) | async-done | bytes 12582928 | tf_op jit(solution)/shard_map/psum | solution.py:78
  308.0 8.4 %fusion.11 = bf16[192,8,16,128]{3,1,2,0:T(8,128)(2,1)} fusion(f32[1536,2048]{1,0:T(8,128)} %all-reduce.3.cloned.1.call-done, f32[1536]{0:T(1024)S(1)} %add_rsqrt_fusion), kind=kLoop, calls=%fused_computation.29 | loop fusion | flops 6291456 | bytes 18880512
  316.4 7.8 %copy.38 = bf16[192,8,16,128]{3,2,1,0:T(8,128)(2,1)} copy(bf16[192,8,16,128]{3,1,2,0:T(8,128)(2,1)} %fusion.11) | data formatting | bytes 12582912
  324.2 37.6 %while.11 = (s32[]{:T(128)}, bf16[3,512,16,128]{3,2,1,0:T(8,128)(2,1)}, s32[3,512]{1,0:T(4,128)S(1)}, bf16[3,512,16,128]{3,2,1,0:T(8,128)(2,1)}, bf16[256,16,128...) while((s32[]{:T(128)}, bf16[3,512,16,128]{3,2,1,0:T(8,128)(2,1)}, ...), condition=%wide.region_8.9_spmd.clone, body=%wide.region_5.8_spmd.clone.sunk | while | flops 1104268288 | bytes 40548948 | solution.py:116
  324.2 0.1 broadcast_compare_fusion.2
  324.3 2.0 constant_dynamic-slice_fusion.5
  326.3 2.4 fusion.50
  328.7 1.8 convert_reduce_fusion.3
  330.5 3.5 fusion.51
  334.0 2.7 copy_dynamic-update-slice_fusion.2
  336.7 0.1 broadcast_compare_fusion.2
  336.9 2.0 constant_dynamic-slice_fusion.5
  338.8 2.4 fusion.50
  341.2 1.8 convert_reduce_fusion.3
  343.1 3.5 fusion.51
  346.5 2.7 copy_dynamic-update-slice_fusion.2
  349.2 0.1 broadcast_compare_fusion.2
  349.4 2.0 constant_dynamic-slice_fusion.5
  351.3 2.4 fusion.50
  353.7 1.8 convert_reduce_fusion.3
  355.6 3.5 fusion.51
  359.0 2.7 copy_dynamic-update-slice_fusion.2
  361.7 18.9 %convolution_convert_fusion = bf16[1536,2048]{1,0:T(8,128)(2,1)} fusion(bf16[2048,2048]{1,0:T(8,128)(2,1)} %param.27, bf16[192,8,16,128]{3,2,1,0:T(8,128)(2,1)} %bitcast.20), kind=kOutput, calls=%fused_computation.28 | convolution fusion | flops 12888047616 | bytes 20971520 | tf_op jit(solution)/shard_map/dot_general | solution.py:117
  380.6 0.0 all-reduce.5.cloned.1.call-update
  380.6 0.7 copy-done.6
  381.3 222.5 %all-reduce.5.cloned.1.call-done = bf16[1536,2048]{1,0:T(8,128)(2,1)} async-done(((bf16[1536,2048]{1,0:T(8,128)(2,1)}), bf16[1536,2048]{1,0:T(8,128)(2,1)}) %all-reduce.5.cloned.1.call-update) | async-done | bytes 6291472 | tf_op jit(solution)/shard_map/psum | solution.py:119
  603.9 12.6 %convert_add_fusion = f32[1536,2048]{1,0:T(8,128)} fusion(bf16[1536,2048]{1,0:T(8,128)(2,1)} %param.22, bf16[1536,2048]{1,0:T(8,128)(2,1)} %all-reduce.5.cloned.1.call-done, f32[2048]{0:T(1024)S(1)} %tanh.3), kind=kLoop, calls=%fused_computation.22 | loop fusion | flops 12582912 | bytes 25174016 | tf_op jit(solution)/shard_map/add | solution.py:120
  (26 shorter events, 0.1 us)
Async XLA Ops:
  7.2 1.5 copy-start
  7.2 36.4 %copy-start.4 = (bf16[64,1280]{1,0:T(8,128)(2,1)S(1)}, bf16[64,1280]{1,0:T(8,128)(2,1)}, u32[]{:S(2)}) copy-start(bf16[64,1280]{1,0:T(8,128)(2,1)} %param.17) | copy-start | bytes 491524
  7.2 8.4 %copy-start.3 = (bf16[384,1280]{1,0:T(8,128)(2,1)S(1)}, bf16[384,1280]{1,0:T(8,128)(2,1)}, u32[]{:S(2)}) copy-start(bf16[384,1280]{1,0:T(8,128)(2,1)} %param.21) | copy-start | bytes 2949124
  7.2 75.8 %all-gather.5.cloned.1.call-start = ((), (), s32[]{:S(2)}) async-start(), calls=%async_computation.2 | async-start | bytes 1310720 | tf_op jit(solution)/shard_map/all_gather | solution.py:88
  14.2 33.8 %copy-start.7 = (bf16[2048]{0:T(1024)(128)(2,1)S(1)}, bf16[2048]{0:T(1024)(128)(2,1)}, u32[]{:S(2)}) copy-start(bf16[2048]{0:T(1024)(128)(2,1)} %param.23) | copy-start | bytes 12292
  15.8 10.8 %collective-permute-start = (f32[64,1280]{1,0:T(8,128)S(1)}, f32[64,1280]{1,0:T(8,128)S(1)}, u32[]{:S(2)}, u32[]{:S(2)}) collective-permute-start(f32[64,1280]{1,0:T(8,128)S(1)} %fusion.25), channel_id=1, source_target_pairs={{0,1},{1,0},{2,3},{3,2},{4,5},{5,4},{6,7},{7,6},{8,9},{9,8},{10,11... | collective-permute-start | bytes 983048 | tf_op jit(solution)/shard_map/ppermute | solution.py:68
  26.7 16.9 %collective-permute-start.1 = (f32[64,1280]{1,0:T(8,128)S(1)}, f32[64,1280]{1,0:T(8,128)S(1)}, u32[]{:S(2)}, u32[]{:S(2)}) collective-permute-start(f32[64,1280]{1,0:T(8,128)S(1)} %add.30), channel_id=1, source_target_pairs={{0,2},{1,3},{2,0},{3,1},{4,6},{5,7},{6,4},{7,5},{8,10},{9,11},{10,... | collective-permute-start | bytes 983048 | tf_op jit(solution)/shard_map/ppermute | solution.py:68
  43.6 27.7 %copy-start.2 = (bf16[64,1280]{1,0:T(8,128)(2,1)}, bf16[64,1280]{1,0:T(8,128)(2,1)S(1)}, u32[]{:S(2)}) copy-start(bf16[64,1280]{1,0:T(8,128)(2,1)S(1)} %add_convert_fusion) | copy-start | bytes 491524
  47.9 36.5 %all-gather.3.cloned.1.call-start = ((), (), s32[]{:S(2)}) async-start(), calls=%async_computation.1 | async-start | bytes 1310720 | tf_op jit(solution)/shard_map/all_gather | solution.py:87
  52.2 255.8 %all-reduce.3.cloned.1.call-start = ((), (), s32[]{:S(2)}) async-start(), calls=%async_computation | async-start | bytes 25165824 | tf_op jit(solution)/shard_map/psum | solution.py:78
  71.3 0.7 copy-start.5
  71.3 532.5 %all-reduce.5.cloned.1.call-start = ((), (), s32[]{:S(2)}) async-start(), calls=%async_computation.3 | async-start | bytes 12582912 | tf_op jit(solution)/shard_map/psum | solution.py:119
  380.6 0.7 copy-start.6
  603.9 12.6 %copy-start.1 = (bf16[1280,384]{1,0:T(8,128)(2,1)S(1)}, bf16[1280,384]{1,0:T(8,128)(2,1)}, u32[]{:S(2)}) copy-start(bf16[1280,384]{1,0:T(8,128)(2,1)} %param.19) | copy-start | bytes 2949124
Sparse Core Ops, SparseCore 0:
  48.1 17.7 all-gather.4
  67.4 16.9 all-gather.2
  87.4 220.5 all-reduce.2
  380.8 223.0 all-reduce.4
